TPU v7x, 32 devices: a whole 2x2x4 slice. The times are simulated.
32 devices in a mesh: ens: 2 (over y), lat: 4 (over x, core), lon: 4 (over z).
Axes of the slice: x: 2, y: 2, z: 4, core: 2. Of those that a mesh axis runs over, the one named last changes fastest.
Arguments:
- tokens: bfloat16 [176, 44, 1024], P(('ens', 'lat'), 'lon'), parts along dimension 0, may hold values from -6 to 6
- qkv_weight: bfloat16 [2, 1024, 1280], P(None, None, 'lon'), may hold values from -4 to 4
- out_weight: bfloat16 [2, 1024, 1024], P(None, None, 'lon'), may hold values from -0.1875 to 0.1875
- norm_gain: float32 [2, 1024], replicated, may hold values from 0.5 to 1.5
- conv_weight: bfloat16 [9, 1024], replicated, may hold values from -4 to 4
- conv_bias: bfloat16 [1024], replicated, may hold values from -6 to 6
Outputs:
- result: bfloat16 [176, 44, 1024], P(('ens', 'lat'), 'lon'), parts along dimension 0
There are 2 independent parts, one for each index of `ens`. A program takes and returns all parts, laid end to end along the dimension named above; an argument that names none is the same for every part. Nothing has to cross between parts.
All inputs are finite; a program needn't handle non-finite values.
Results may differ from a plain program's by a relative error of at most 0.04.
Values may be sent and summed in bfloat16 or wider, within the bound.
A program may use at most 64 MiB of HBM per device.

v0:
```python
import jax
import jax.numpy as jnp
from jax import lax
from jax.sharding import PartitionSpec as P

HEADS = 16
KV = 2
HD = 64


def with_halo(cells, sides, width, closed):
    for axis, dim in sides:
        count = lax.axis_size(axis)
        ends = count if closed else count - 1
        head = lax.slice_in_dim(cells, 0, width, axis=dim)
        tail = lax.slice_in_dim(cells, cells.shape[dim] - width, cells.shape[dim], axis=dim)
        cells = jnp.concatenate(
            [
                lax.ppermute(tail, axis, [(i, (i + 1) % count) for i in range(ends)]),
                cells,
                lax.ppermute(head, axis, [((i + 1) % count, i) for i in range(ends)]),
            ],
            axis=dim,
        )
    return cells


def split_keyval(keyval):
    batch, length, columns = keyval.shape
    keys = keyval[..., : KV * HD].reshape(batch, length, KV, HD)
    values = keyval[..., KV * HD :].reshape(batch, length, KV, HD)
    return (keys, values)


def line_scores(query, keys):
    batch, length, feature = query.shape
    grouped = query.reshape(batch, length, KV, HEADS // KV, HD)
    return jnp.einsum(
        "nqgjd,nkgd->ngjqk", grouped, keys, preferred_element_type=jnp.float32
    ) * HD ** (-0.5)


def attend_lines(query, keyval):
    batch, length, feature = query.shape
    keys, values = split_keyval(keyval)
    scores = line_scores(query, keys)
    peak = jnp.max(scores, axis=-1, keepdims=True)
    expon = jnp.exp(scores - peak)
    denominator = jnp.sum(expon, axis=-1)
    mixed = jnp.einsum(
        "ngjqk,nkgd->nqgjd", expon.astype(jnp.bfloat16), values, preferred_element_type=jnp.float32
    )
    mixed = mixed / jnp.transpose(denominator, (0, 3, 1, 2))[..., None]
    return mixed.reshape(batch, length, feature).astype(jnp.bfloat16)


def rms_norm(current, gain):
    values = current.astype(jnp.float32)
    scaled = values * lax.rsqrt(jnp.mean(values * values, axis=-1, keepdims=True) + 1e-06)
    return (scaled * gain).astype(jnp.bfloat16)


def shards(tokens, qkv_weight, out_weight, norm_gain, conv_weight, conv_bias):
    lat_rows, lon_cols, feature = tokens.shape
    widened = with_halo(tokens, (("lon", 1),), 1, True)
    padded = with_halo(widened, (("lat", 0),), 1, False)
    total = tokens.astype(jnp.float32) + conv_bias.astype(jnp.float32)
    for shift_lat in range(3):
        for shift_lon in range(3):
            window = padded[
                shift_lat : shift_lat + lat_rows, shift_lon : shift_lon + lon_cols
            ].astype(jnp.float32)
            total = total + conv_weight[3 * shift_lat + shift_lon].astype(jnp.float32) * window
    current = total.astype(jnp.bfloat16)
    for section_index in range(2):
        weight_in, weight_out = (
            lax.all_gather(qkv_weight[section_index], "lon", axis=1, tiled=True),
            lax.all_gather(out_weight[section_index], "lon", axis=1, tiled=True),
        )
        normed = rms_norm(current, norm_gain[section_index])
        projected = jnp.dot(
            normed.reshape(-1, feature), weight_in, preferred_element_type=jnp.float32
        )
        projected = projected.astype(jnp.bfloat16).reshape(lat_rows, lon_cols, -1)
        query = projected[..., :feature]
        keyval = projected[..., feature:]
        if section_index == 0:
            gathered = lax.all_gather(keyval, "lon", axis=1, tiled=True)
            attended = attend_lines(query, gathered)
        else:
            gathered = lax.all_gather(keyval, "lat", axis=0, tiled=True)
            attended = attend_lines(
                jnp.transpose(query, (1, 0, 2)), jnp.transpose(gathered, (1, 0, 2))
            )
            attended = jnp.transpose(attended, (1, 0, 2))
        output = jnp.dot(
            attended.reshape(-1, feature), weight_out, preferred_element_type=jnp.float32
        )
        current = (
            current.astype(jnp.float32) + output.reshape(lat_rows, lon_cols, feature)
        ).astype(jnp.bfloat16)
    return current


def solution(mesh):
    in_specs = (
        P(("ens", "lat"), "lon", None),
        P(None, None, "lon"),
        P(None, None, "lon"),
        P(),
        P(),
        P(),
    )
    out_specs = P(("ens", "lat"), "lon", None)
    return jax.shard_map(shards, mesh=mesh, in_specs=in_specs, out_specs=out_specs, check_vma=False)
```

profile of v0, /device:TPU:0, one launch (start us, length us, event | category | flops | bytes accessed | tf_op | source)
XLA Modules:
  0.0 230.8 jit_solution(9148492533979211123)
XLA Ops:
  6.5 2.6 %fusion.68 = (bf16[1,1024,320]{1,2,0:T(8,128)(2,1)}, bf16[1,1024,320]{1,2,0:T(8,128)(2,1)}) fusion(bf16[2,1024,320]{1,2,0:T(8,128)(2,1)} %param.7), kind=kLoop, calls=%fused_computation.94 | loop fusion | bytes 2621440 | tf_op jit(solution)/shard_map/slice | solution.py:77
  9.2 1.0 fusion.69
  11.3 3.1 %collective-permute-start = (bf16[22,1,1024]{2,0,1:T(8,128)(2,1)S(1)}, bf16[22,1,1024]{2,0,1:T(8,128)(2,1)S(1)}, u32[]{:S(2)}, u32[]{:S(2)}) collective-permute-start(bf16[22,1,1024]{2,0,1:T(8,128)(2,1)S(1)} %get-tuple-element.18), channel_id=1, source_target_pairs={{0,1},{1,2},{2,3},{3,0},{4,5},{5,6},{6,7},{7,4},{8,9},{9,10},{10,1... | collective-permute-start | bytes 135176 | tf_op jit(solution)/shard_map/ppermute | solution.py:19
  14.4 2.1 collective-permute-start.1
  16.5 2.0 collective-permute-done
  19.1 1.3 collective-permute-start.2
  20.4 1.3 collective-permute-start.3
  21.8 3.5 %collective-permute-done.3 = bf16[1,13,1024]{2,0,1:T(2,128)(2,1)S(1)} collective-permute-done((bf16[1,13,1024]{2,0,1:T(2,128)(2,1)S(1)}, bf16[1,13,1024]{2,0,1:T(2,128)(2,1)S(1)}, u32[]{:S(2)}, u32[]{:S(2)}) %collective-permute-start.3) | collective-permute-done | bytes 26656 | tf_op jit(solution)/shard_map/ppermute | solution.py:21
  25.3 2.4 %fusion.47 = (f32[22,11]{0,1:T(8,128)S(1)}, bf16[22,11,1024]{2,0,1:T(8,128)(2,1)S(1)}) fusion(bf16[1,13,1024]{2,0,1:T(2,128)(2,1)S(1)} %collective-permute-done.3, bf16[22,13,1024]{2,0,1:T(8,128)(2,1)S(1)} %constant_dynamic-update-slice_fusion, f32[1024]{0:T(1024)S(1)} %bitcast.118, f32[1024]{0:T(1024)S(1)} %bitcast.119, f32[1024]{0:T(1024)S(1)} %bitcast.112, ...), kind=kLoop, calls=%fused_computation.48 | loop fusion | flops 13877006 | bytes 1762248 | tf_op jit(solution)/shard_map/reduce_sum | solution.py:59
  28.4 38.4 %all-gather.9.cloned.1.call-done = bf16[1,1024,1280]{1,2,0:T(8,128)(2,1)} async-done(((bf16[1,1024,320]{1,2,0:T(8,128)(2,1)}), bf16[1,1024,1280]{1,2,0:T(8,128)(2,1)}) %all-gather.9.cloned.1.call-update) | async-done | bytes 2621456 | tf_op jit(solution)/shard_map/all_gather | solution.py:77
  66.8 2.6 %fusion.6 = bf16[242,1280]{1,0:T(8,128)(2,1)S(1)} fusion(bf16[242,1024]{1,0:T(8,128)(2,1)S(1)} %reshape.129, bf16[1,1024,1280]{1,2,0:T(8,128)(2,1)} %all-gather.9.cloned.1.call-done), kind=kOutput, calls=%fused_computation.9 | convolution fusion | flops 634698240 | bytes 3736576 | tf_op jit(solution)/shard_map/dot_general | solution.py:81
  69.7 24.8 %all_gather.19 = bf16[22,44,256]{2,0,1:T(8,128)(2,1)S(1)} all-gather(bf16[22,11,256]{2,0,1:T(8,128)(2,1)S(1)} %copy.22), channel_id=1, replica_groups=mesh['ens'=2,'lat'=4,'lon'=4] {'lon'}, dimensions={1}, use_global_device_ids=true | all-gather | bytes 619520 | tf_op jit(solution)/shard_map/all_gather | solution.py:88
  96.7 1.0 bitcast_reduce_fusion
  97.7 1.8 fusion.12
  99.4 2.0 fusion
  102.4 17.7 %all-gather.11.cloned.1.call-done = bf16[1,1024,1024]{2,1,0:T(8,128)(2,1)} async-done(((bf16[1,1024,256]{2,1,0:T(8,128)(2,1)}), bf16[1,1024,1024]{2,1,0:T(8,128)(2,1)}) %all-gather.11.cloned.1.call-update) | async-done | bytes 2097168 | tf_op jit(solution)/shard_map/all_gather | solution.py:78
  120.1 2.5 %fusion.50 = (f32[22,11]{0,1:T(8,128)S(1)}, bf16[22,11,1024]{2,0,1:T(8,128)(2,1)S(1)}) fusion(bf16[22,11,1024]{2,0,1:T(8,128)(2,1)S(1)} %convert_element_type.204, bf16[1,1024,1024]{2,1,0:T(8,128)(2,1)} %all-gather.11.cloned.1.call-done, bf16[22,11,1024]{2,0,1:T(8,128)(2,1)S(1)} %get-tuple-element.6), kind=kOutput, calls=%fused_computation.51 | convolution fusion | flops 508997376 | bytes 3584968 | tf_op jit(solution)/shard_map/dot_general | solution.py:96
  123.2 51.5 %all-gather.13.cloned.1.call-done = bf16[1,1024,1280]{1,2,0:T(8,128)(2,1)} async-done(((bf16[1,1024,320]{1,2,0:T(8,128)(2,1)}), bf16[1,1024,1280]{1,2,0:T(8,128)(2,1)}) %all-gather.13.cloned.1.call-update) | async-done | bytes 2621456 | tf_op jit(solution)/shard_map/all_gather | solution.py:77
  174.7 2.6 %fusion.9 = bf16[242,1280]{1,0:T(8,128)(2,1)S(1)} fusion(bf16[242,1024]{1,0:T(8,128)(2,1)S(1)} %reshape.134, bf16[1,1024,1280]{1,2,0:T(8,128)(2,1)} %all-gather.13.cloned.1.call-done), kind=kOutput, calls=%fused_computation.10 | convolution fusion | flops 634698240 | bytes 3736576 | tf_op jit(solution)/shard_map/dot_general | solution.py:81
  177.6 8.4 %all_gather.22 = bf16[88,11,256]{2,1,0:T(8,128)(2,1)S(1)} all-gather(bf16[22,11,256]{2,1,0:T(8,128)(2,1)S(1)} %slice.162), channel_id=1, replica_groups=mesh['ens'=2,'lat'=4,'lon'=4] {'lat'}, dimensions={0}, use_global_device_ids=true | all-gather | bytes 619520 | tf_op jit(solution)/shard_map/all_gather | solution.py:91
  188.3 1.4 fusion.20
  189.7 1.4 fusion.14
  192.0 29.1 %all-gather.15.cloned.1.call-done = bf16[1,1024,1024]{2,1,0:T(8,128)(2,1)} async-done(((bf16[1,1024,256]{2,1,0:T(8,128)(2,1)}), bf16[1,1024,1024]{2,1,0:T(8,128)(2,1)}) %all-gather.15.cloned.1.call-update) | async-done | bytes 2097168 | tf_op jit(solution)/shard_map/all_gather | solution.py:78
  221.2 3.1 %fusion.34 = bf16[22,11,1024]{2,0,1:T(8,128)(2,1)} fusion(bf16[1,1024,1024]{2,1,0:T(8,128)(2,1)} %all-gather.15.cloned.1.call-done, bf16[22,11,1024]{2,0,1:T(8,128)(2,1)S(1)} %get-tuple-element.33, bf16[11,22,1024]{2,1,0:T(8,128)(2,1)S(1)} %convert_element_type.211), kind=kOutput, calls=%fused_computation.37 | convolution fusion | flops 508254208 | bytes 3584000 | tf_op jit(solution)/shard_map/dot_general | solution.py:96
  (59 shorter events, 9.8 us)
Async XLA Ops:
  6.5 2.6 %copy-start.2 = (bf16[2,1024,256]{2,1,0:T(8,128)(2,1)S(1)}, bf16[2,1024,256]{2,1,0:T(8,128)(2,1)}, u32[]{:S(2)}) copy-start(bf16[2,1024,256]{2,1,0:T(8,128)(2,1)} %param.8) | copy-start | bytes 3145732
  6.5 60.3 %all-gather.9.cloned.1.call-start = ((), (), s32[]{:S(2)}) async-start(), calls=%async_computation | async-start | bytes 3276800 | tf_op jit(solution)/shard_map/all_gather | solution.py:77
  9.1 110.9 %all-gather.11.cloned.1.call-start = ((), (), s32[]{:S(2)}) async-start(), calls=%async_computation.1 | async-start | bytes 2621440 | tf_op jit(solution)/shard_map/all_gather | solution.py:78
  10.2 1.0 copy-start.1
  10.2 6.3 %copy-start.3 = (bf16[9,1024]{1,0:T(8,128)(2,1)S(1)}, bf16[9,1024]{1,0:T(8,128)(2,1)}, u32[]{:S(2)}) copy-start(bf16[9,1024]{1,0:T(8,128)(2,1)} %param.10) | copy-start | bytes 55300
  10.3 164.4 %all-gather.13.cloned.1.call-start = ((), (), s32[]{:S(2)}) async-start(), calls=%async_computation.2 | async-start | bytes 3276800 | tf_op jit(solution)/shard_map/all_gather | solution.py:77
  11.0 210.2 %all-gather.15.cloned.1.call-start = ((), (), s32[]{:S(2)}) async-start(), calls=%async_computation.3 | async-start | bytes 2621440 | tf_op jit(solution)/shard_map/all_gather | solution.py:78
  11.3 10.4 %copy-start.4 = (f32[2,1024]{1,0:T(2,128)S(1)}, f32[2,1024]{1,0:T(2,128)}, u32[]{:S(2)}) copy-start(f32[2,1024]{1,0:T(2,128)} %param.9) | copy-start | bytes 24580
  11.3 10.4 %copy-start.5 = (bf16[1024]{0:T(1024)(128)(2,1)S(1)}, bf16[1024]{0:T(1024)(128)(2,1)}, u32[]{:S(2)}) copy-start(bf16[1024]{0:T(1024)(128)(2,1)} %param.11) | copy-start | bytes 6148
  11.3 7.3 %collective-permute-start = (bf16[22,1,1024]{2,0,1:T(8,128)(2,1)S(1)}, bf16[22,1,1024]{2,0,1:T(8,128)(2,1)S(1)}, u32[]{:S(2)}, u32[]{:S(2)}) collective-permute-start(bf16[22,1,1024]{2,0,1:T(8,128)(2,1)S(1)} %get-tuple-element.18), channel_id=1, source_target_pairs={{0,1},{1,2},{2,3},{3,0},{4,5},{5,6},{6,7},{7,4},{8,9},{9,10},{10,1... | collective-permute-start | bytes 135176 | tf_op jit(solution)/shard_map/ppermute | solution.py:19
  14.4 4.6 %collective-permute-start.1 = (bf16[22,1,1024]{2,0,1:T(8,128)(2,1)S(1)}, bf16[22,1,1024]{2,0,1:T(8,128)(2,1)S(1)}, u32[]{:S(2)}, u32[]{:S(2)}) collective-permute-start(bf16[22,1,1024]{2,0,1:T(8,128)(2,1)S(1)} %get-tuple-element.17), channel_id=1, source_target_pairs={{1,0},{2,1},{3,2},{0,3},{5,4},{6,5},{7,6},{4,7},{9,8},{10,9},{11,1... | collective-permute-start | bytes 135176 | tf_op jit(solution)/shard_map/ppermute | solution.py:21
  19.1 2.7 %collective-permute-start.2 = (bf16[1,13,1024]{2,0,1:T(2,128)(2,1)S(1)}, bf16[1,13,1024]{2,0,1:T(2,128)(2,1)S(1)}, u32[]{:S(2)}, u32[]{:S(2)}) collective-permute-start(bf16[1,13,1024]{2,0,1:T(2,128)(2,1)S(1)} %get-tuple-element.13), channel_id=1, source_target_pairs={{0,4},{4,8},{8,12},{1,5},{5,9},{9,13},{2,6},{6,10},{10,14},{3,7},{... | collective-permute-start | bytes 79880 | tf_op jit(solution)/shard_map/ppermute | solution.py:19
  20.4 4.9 %collective-permute-start.3 = (bf16[1,13,1024]{2,0,1:T(2,128)(2,1)S(1)}, bf16[1,13,1024]{2,0,1:T(2,128)(2,1)S(1)}, u32[]{:S(2)}, u32[]{:S(2)}) collective-permute-start(bf16[1,13,1024]{2,0,1:T(2,128)(2,1)S(1)} %get-tuple-element.14), channel_id=1, source_target_pairs={{4,0},{8,4},{12,8},{5,1},{9,5},{13,9},{6,2},{10,6},{14,10},{7,3},{... | collective-permute-start | bytes 79880 | tf_op jit(solution)/shard_map/ppermute | solution.py:21
  69.7 24.9 %copy-start = (bf16[22,11,1280]{2,1,0:T(8,128)(2,1)}, bf16[22,11,1280]{2,1,0:T(8,128)(2,1)S(1)}, u32[]{:S(2)}) copy-start(bf16[22,11,1280]{2,1,0:T(8,128)(2,1)S(1)} %reshape.130) | copy-start | bytes 1858564
  94.6 1.1 slice-start
Sparse Core Ops, SparseCore 0:
  9.2 57.4 all-gather.8
  68.3 51.6 all-gather.10
  121.6 53.0 all-gather.12
  176.1 44.9 all-gather.14
where the time goes:
time: 231 us
  waiting for transfers between devices  143 us (62%)
  blocking collectives  33.2 us (14%)
  matrix products  16 us (7%)
  between operations  13.5 us (6%)
  local copies, waits for them, and re-layouts  11 us (5%)
  starting transfers between devices  7.88 us (3%)
  other arithmetic  6 us (3%)
    all_gather x2, waiting for transfers between devices, shards(): lax.all_gather(qkv_weight[section_index], 'lon', axis=1, tiled=True)  89.9 us
    all_gather x2, waiting for transfers between devices, shards(): lax.all_gather(out_weight[section_index], 'lon', axis=1, tiled=True)  46.8 us
    all_gather x1, blocking collectives, shards(): gathered = lax.all_gather(keyval, 'lon', axis=1, tiled=True)  24.8 us
    all_gather x1, blocking collectives, shards(): gathered = lax.all_gather(keyval, 'lat', axis=0, tiled=True)  8.4 us
    dot_general x2, matrix products, shards(): jnp.dot(attended.reshape(-1, feature), weight_out, preferred_element_type...  5.6 us
    dot_general x2, matrix products, shards(): jnp.dot(normed.reshape(-1, feature), weight_in, preferred_element_type=jn...  5.24 us
  transfers between devices with their start and end apart: 8, of which 7 were waited for; matrix products, arithmetic and copies ran while one was open for 11% of the time, Pallas kernels for 0%

commit v1 on v0

--- a/solution.py
+++ b/solution.py
@@ -1,6 +1,10 @@
+import functools
+
 import jax
 import jax.numpy as jnp
 from jax import lax
+from jax.experimental import pallas as pl
+from jax.experimental.pallas import tpu as pltpu
 from jax.sharding import PartitionSpec as P
 
 HEADS = 16
@@ -102,6 +106,327 @@
     return current
 
 
+MESH = pl.DeviceIdType.MESH
+F32 = jnp.float32
+BF16 = jnp.bfloat16
+PLANE = 8
+
+
+def remote(src, dst, send, recv, device):
+    return pltpu.make_async_remote_copy(
+        src_ref=src, dst_ref=dst, send_sem=send, recv_sem=recv, device_id=device, device_id_type=MESH
+    )
+
+
+def step_kernel(
+    nlat, nlon, tokens, wq_in, wo_in, gain, conv_w, conv_b, out,
+    wq, wo, pad, colf, col, hcol, hrow, hcor, cur, normed, proj, att, kv0, kv1,
+    sem_w, sem_z, sem_f, sem_c, sem_hs, sem_hr, sem_ks, sem_kr, sem_l,
+):
+    rows, cols, feature = tokens.shape
+    step0, step1 = 16, 32
+    count = rows * step0
+    ens, lat, lon = lax.axis_index("ens"), lax.axis_index("lat"), lax.axis_index("lon")
+    here = ens * 4 + lax.rem(lat, 4)
+
+    def flip(value, bit):
+        return value + bit - 2 * bit * lax.rem(value // bit, 2)
+
+    piece = feature // PLANE
+    dev_core = (ens, flip(lat, 1), lon)
+    dev_x = (ens, flip(lat, 2), lon)
+    dev_y = (1 - ens, lat, lon)
+    dev_xy = (1 - ens, flip(lat, 2), lon)
+    p_core, p_x, p_y = flip(here, 1), flip(here, 2), flip(here, 4)
+    p_xy = flip(p_x, 4)
+    far = [lax.rem(lon + d, nlon) for d in range(nlon)]
+    farlat = [lax.rem(lat + d, nlat) for d in range(nlat)]
+
+    def part(m, s, p):
+        buf = wo if m % 2 else wq
+        return buf.at[m // 2, s, pl.ds(pl.multiple_of(p * piece, piece), piece), :]
+
+    def own(m):
+        return (wo_in if m % 2 else wq_in).at[m // 2]
+
+    barrier = pltpu.get_barrier_semaphore()
+    greet = [(ens, lat, far[d]) for d in range(1, nlon)]
+    greet += [(ens, farlat[d], lon) for d in range(1, nlat)]
+    greet += [(ens, farlat[a], far[b]) for a in (1, nlat - 1) for b in (1, nlon - 1)]
+    greet += [dev_y, dev_xy]
+    for device in greet:
+        pl.semaphore_signal(barrier, inc=1, device_id=device, device_id_type=MESH)
+    pl.semaphore_wait(barrier, len(greet))
+
+    pending, kv_sends = [], []
+
+    def launch(copy):
+        copy.start()
+        pending.append(copy)
+
+    def send_z(m):
+        for d in range(1, nlon):
+            launch(remote(
+                own(m).at[pl.ds(pl.multiple_of(here * piece, piece), piece), :],
+                part(m, lon, here), sem_z.at[m, d], sem_w.at[m, lon, here], (ens, lat, far[d]),
+            ))
+
+    def arrived(m, s, p):
+        remote(part(m, s, p), part(m, s, p), sem_z.at[m, 0], sem_w.at[m, s, p], dev_core).wait_recv()
+
+    def pass_on(m, s, p, send, device):
+        launch(remote(part(m, s, p), part(m, s, p), send, sem_w.at[m, s, p], device))
+
+    def spread(m):
+        for d in (1, 3, 2) if nlon == 4 else range(1, nlon):
+            arrived(m, far[d], here)
+            pass_on(m, far[d], here, sem_f.at[m, d, 0], dev_x)
+            pass_on(m, far[d], here, sem_f.at[m, d, 1], dev_y)
+            pass_on(m, far[d], here, sem_f.at[m, d, 2], dev_xy)
+            pass_on(m, far[d], here, sem_f.at[m, d, 3], dev_core)
+
+    def share(m):
+        for d in (1, 3, 2) if nlon == 4 else range(1, nlon):
+            for k, p in enumerate((p_x, p_y, p_xy)):
+                arrived(m, far[d], p)
+                pass_on(m, far[d], p, sem_c.at[m, d, k], dev_core)
+
+    def finish(m):
+        pltpu.make_async_copy(own(m), (wo if m % 2 else wq).at[m // 2, lon], sem_l.at[m]).wait()
+        for d in range(1, nlon):
+            for p in (p_core, flip(p_x, 1), flip(p_y, 1), flip(p_xy, 1)):
+                arrived(m, far[d], p)
+
+    send_z(0)
+    for m in range(4):
+        pltpu.make_async_copy(own(m), (wo if m % 2 else wq).at[m // 2, lon], sem_l.at[m]).start()
+
+    colf[...] = jnp.zeros_like(colf)
+    for i in range(rows):
+        row = tokens[i].astype(F32)
+        pad[1 + i, 8 : 8 + cols, :] = row
+        colf[0, i : i + 1, :] = row[0:1]
+        colf[1, i : i + 1, :] = row[cols - 1 : cols]
+    col[...] = colf[...].astype(BF16)
+    low, high = pl.ds(0, 16), pl.ds(16, 16)
+    north, south, west, east = farlat[nlat - 1], farlat[1], far[nlon - 1], far[1]
+    halos = [
+        (col.at[1], hcol.at[0], (ens, lat, east)),
+        (col.at[0], hcol.at[1], (ens, lat, west)),
+        (tokens.at[rows - 1], hrow.at[0], (ens, south, lon)),
+        (tokens.at[0], hrow.at[1], (ens, north, lon)),
+        (col.at[1, high], hcor.at[0], (ens, south, east)),
+        (col.at[0, high], hcor.at[1], (ens, south, west)),
+        (col.at[1, low], hcor.at[2], (ens, north, east)),
+        (col.at[0, low], hcor.at[3], (ens, north, west)),
+    ]
+    hcopies = [remote(a, b, sem_hs.at[k], sem_hr.at[k], dev) for k, (a, b, dev) in enumerate(halos)]
+    for copy in hcopies:
+        launch(copy)
+    for m in (1, 2, 3):
+        send_z(m)
+    spread(0)
+    for copy in hcopies:
+        copy.wait_recv()
+
+    for side, place in ((0, 7), (1, 8 + cols)):
+        edge = hcol[side].astype(F32)
+        for i in range(rows):
+            pad[1 + i, place : place + 1, :] = edge[i : i + 1]
+    last = rows - 1 - 16
+    for k, (index, inside) in enumerate(((0, lat > 0), (rows + 1, lat < nlat - 1))):
+        keep = jnp.where(inside, 1.0, 0.0).astype(F32)
+        pick = last if k == 0 else 0
+        pad[index, 8 : 8 + cols, :] = hrow[k].astype(F32) * keep
+        pad[index, 7:8, :] = hcor[2 * k].astype(F32)[pick : pick + 1] * keep
+        pad[index, 8 + cols : 9 + cols, :] = hcor[2 * k + 1].astype(F32)[pick : pick + 1] * keep
+
+    taps = conv_w[...].astype(F32)
+    bias = conv_b[...].astype(F32)
+    alive = lax.broadcasted_iota(jnp.int32, (step0, 1), 0) < cols
+
+    def rms(values, k):
+        scaled = values * lax.rsqrt(jnp.mean(values * values, axis=-1, keepdims=True) + 1e-06)
+        return (scaled * gain[k : k + 1, :]).astype(BF16)
+
+    def conv_row(i, carry):
+        total = pad[i + 1, 8 : 8 + step0, :] + bias
+        for a in range(3):
+            for b in range(3):
+                total = total + taps[3 * a + b : 3 * a + b + 1] * pad[i + a, 7 + b : 7 + b + step0, :]
+        rounded = jnp.where(alive, total, 0.0).astype(BF16)
+        spot = pl.ds(pl.multiple_of(i * step0, step0), step0)
+        cur[spot, :] = rounded
+        normed[spot, :] = rms(rounded.astype(F32), 0)
+        return carry
+
+    lax.fori_loop(0, rows, conv_row, 0)
+
+    def halves(pair_block):
+        left = lax.broadcasted_iota(jnp.int32, pair_block.shape, 1) < HD
+        swapped = jnp.concatenate([pair_block[:, HD:], pair_block[:, :HD]], axis=1)
+        zero = jnp.zeros_like(pair_block)
+        first = (jnp.where(left, pair_block, zero), jnp.where(left, zero, swapped))
+        second = (jnp.where(left, swapped, zero), jnp.where(left, zero, pair_block))
+        return (first, second)
+
+    def attend(kv, parts, blocks, step, valid):
+        width = parts * step
+        pairs = HEADS // KV // 2
+
+        def body(r, carry):
+            spot = pl.ds(pl.multiple_of(r * step, step), step)
+            keys = jnp.concatenate([kv[s, spot, 0 : KV * HD] for s in range(parts)], axis=0)
+            values = jnp.concatenate([kv[s, spot, KV * HD :] for s in range(parts)], axis=0)
+            kh, vh = halves(keys), halves(values)
+            lane = lax.broadcasted_iota(jnp.int32, (1, width), 1)
+            valid_key = lax.rem(lane, step) < valid
+            left = lax.broadcasted_iota(jnp.int32, (1, 2 * HD), 1) < HD
+            for g in range(KV):
+                base = g * pairs
+                query = jnp.concatenate(
+                    [proj[spot, (base + p) * 128 : (base + p + 1) * 128] for p in range(pairs)], axis=0
+                )
+                mixed, inverse = None, []
+                for half in range(2):
+                    scores = lax.dot_general(
+                        query, kh[g][half], (((1,), (1,)), ((), ())), preferred_element_type=F32
+                    ) * HD ** (-0.5)
+                    scores = jnp.where(valid_key, scores, -jnp.inf)
+                    expon = jnp.exp(scores - jnp.max(scores, axis=-1, keepdims=True))
+                    inverse.append(1.0 / jnp.sum(expon, axis=-1, keepdims=True))
+                    term = jnp.dot(expon.astype(BF16), vh[g][half], preferred_element_type=F32)
+                    mixed = term if mixed is None else mixed + term
+                mixed = (mixed * jnp.where(left, inverse[0], inverse[1])).astype(BF16)
+                for p in range(pairs):
+                    att[spot, (base + p) * 128 : (base + p + 1) * 128] = mixed[p * step : (p + 1) * step]
+            return carry
+
+        lax.fori_loop(0, blocks, body, 0)
+
+    def project(k, which):
+        for t in which:
+            both = [
+                jnp.dot(normed[...], wq[k, s], preferred_element_type=F32).astype(BF16)
+                for s in (2 * t, 2 * t + 1)
+            ]
+            width = both[0].shape[1]
+            proj[:, 2 * t * width : 2 * (t + 1) * width] = jnp.concatenate(both, axis=1)
+
+    def send_kv(k, kv, targets, mine):
+        for d, device in targets:
+            copy = remote(
+                proj.at[:, pl.ds(feature, 2 * KV * HD)], kv.at[mine], sem_ks.at[k, d], sem_kr.at[k, mine], device
+            )
+            copy.start()
+            kv_sends.append(copy)
+        kv[mine] = proj[:, feature:]
+
+    def take_kv(k, kv, sources):
+        for s in sources:
+            remote(kv.at[s], kv.at[s], sem_ks.at[k, 0], sem_kr.at[k, s], dev_core).wait_recv()
+
+    def back(k, values, s, width):
+        lanes = pl.ds(s * width, width)
+        return (cur[:, lanes].astype(F32) + jnp.dot(values, wo[k, s], preferred_element_type=F32)).astype(BF16)
+
+    share(0)
+    spread(1)
+    finish(0)
+    project(0, (1,))
+    send_kv(0, kv0, [(d, (ens, lat, far[d])) for d in range(1, nlon)], lon)
+    project(0, (0,))
+    share(1)
+    spread(2)
+    take_kv(0, kv0, far[1:])
+    attend(kv0, nlon, rows, step0, cols)
+    finish(1)
+    width = wo.shape[3]
+    for s in range(nlon):
+        cur[:, s * width : (s + 1) * width] = back(0, att[...], s, width)
+    share(2)
+    spread(3)
+
+    def norm_row(i, carry):
+        spot = pl.ds(pl.multiple_of(i * step1, step1), step1)
+        att[spot, :] = rms(cur[spot, :].astype(F32), 1)
+        return carry
+
+    lax.fori_loop(0, count // step1, norm_row, 0)
+    to = lax.broadcasted_iota(jnp.int32, (count, count), 0)
+    fro = lax.broadcasted_iota(jnp.int32, (count, count), 1)
+    turn = (fro == lax.rem(to, step1) * step0 + to // step1) & (lax.rem(to, step1) < rows)
+    normed[...] = jnp.dot(turn.astype(F32).astype(BF16), att[...], preferred_element_type=F32).astype(BF16)
+    for copy in kv_sends:
+        copy.wait_send()
+    finish(2)
+    project(1, (1,))
+    send_kv(1, kv1, [(d, (ens, farlat[d], lon)) for d in range(1, nlat)], lat)
+    project(1, (0,))
+    share(3)
+    take_kv(1, kv1, farlat[1:])
+    attend(kv1, nlat, cols, step1, rows)
+    unturn = (fro == lax.rem(to, step0) * step1 + to // step0) & (lax.rem(to, step0) < cols)
+    normed[...] = jnp.dot(unturn.astype(F32).astype(BF16), att[...], preferred_element_type=F32).astype(BF16)
+    finish(3)
+    for s in range(nlon):
+        done = back(1, normed[...], s, width)
+        out[:, :, s * width : (s + 1) * width] = done.reshape(rows, step0, width)[:, :cols, :]
+    for copy in pending + kv_sends[nlon - 1 :]:
+        copy.wait_send()
+
+
+def fused(tokens, qkv_weight, out_weight, norm_gain, conv_weight, conv_bias, nlat, nlon):
+    rows, cols, feature = tokens.shape
+    count = rows * 16
+    vmem = pl.BlockSpec(memory_space=pltpu.VMEM)
+    hbm = pl.BlockSpec(memory_space=pl.ANY)
+    dma = pltpu.SemaphoreType.DMA
+    return pl.pallas_call(
+        functools.partial(step_kernel, nlat, nlon),
+        out_shape=jax.ShapeDtypeStruct(tokens.shape, BF16),
+        in_specs=[vmem, hbm, hbm, vmem, vmem, vmem],
+        out_specs=vmem,
+        scratch_shapes=[
+            pltpu.VMEM((2, nlon) + qkv_weight.shape[1:], BF16),
+            pltpu.VMEM((2, nlon) + out_weight.shape[1:], BF16),
+            pltpu.VMEM((rows + 2, 32, feature), F32),
+            pltpu.VMEM((2, 32, feature), F32),
+            pltpu.VMEM((2, 32, feature), BF16),
+            pltpu.VMEM((2, 32, feature), BF16),
+            pltpu.VMEM((2, cols, feature), BF16),
+            pltpu.VMEM((4, 16, feature), BF16),
+            pltpu.VMEM((count, feature), BF16),
+            pltpu.VMEM((count, feature), BF16),
+            pltpu.VMEM((count, feature + 2 * KV * HD), BF16),
+            pltpu.VMEM((count, feature), BF16),
+            pltpu.VMEM((nlon, count, 2 * KV * HD), BF16),
+            pltpu.VMEM((nlat, count, 2 * KV * HD), BF16),
+            dma((4, nlon, PLANE)),
+            dma((4, nlon)),
+            dma((4, nlon, 4)),
+            dma((4, nlon, 3)),
+            dma((8,)),
+            dma((8,)),
+            dma((2, max(nlat, nlon))),
+            dma((2, max(nlat, nlon))),
+            dma((4,)),
+        ],
+        compiler_params=pltpu.CompilerParams(
+            collective_id=0, has_side_effects=True, vmem_limit_bytes=56 * 2**20
+        ),
+    )(tokens, qkv_weight, out_weight, norm_gain, conv_weight, conv_bias.reshape(1, feature))
+
+
+def entry(tokens, qkv_weight, out_weight, norm_gain, conv_weight, conv_bias):
+    nens, nlat, nlon = (lax.axis_size(name) for name in ("ens", "lat", "lon"))
+    if (nens, nlat, nlon) == (2, 4, 4) and tokens.shape[:2] == (22, 11):
+        return fused(
+            tokens, qkv_weight, out_weight, norm_gain, conv_weight, conv_bias, nlat, nlon
+        )
+    return shards(tokens, qkv_weight, out_weight, norm_gain, conv_weight, conv_bias)
+
+
 def solution(mesh):
     in_specs = (
         P(("ens", "lat"), "lon", None),
@@ -112,4 +437,4 @@
         P(),
     )
     out_specs = P(("ens", "lat"), "lon", None)
-    return jax.shard_map(shards, mesh=mesh, in_specs=in_specs, out_specs=out_specs, check_vma=False)
+    return jax.shard_map(entry, mesh=mesh, in_specs=in_specs, out_specs=out_specs, check_vma=False)

time: 231 us -> 111 us (0.48)
  the two profiles are of different devices: /device:TPU:0 before, /device:TPU:13 now
where the time goes in v1:
time: 111 us
  Pallas kernels  102 us (92%)
  local copies, waits for them, and re-layouts  8.25 us (7%)
    pallas_call x1, Pallas kernels, fused(): pl.pallas_call(functools.partial(step_kernel, nlat, nlon), out_shape=jax....  102 us
    unnamed x2, local copies, waits for them, and re-layouts  4.76 us

profile of v1, /device:TPU:13, one launch (start us, length us, event | category | flops | bytes accessed | tf_op | source)
XLA Modules:
  0.0 110.6 jit_solution(7186191790728168752)
XLA Ops:
  0.0 1.3 %reshape.3.conv_b = bf16[1,1024]{1,0:T(2,128)(2,1)} reshape(bf16[1024]{0:T(1024)(128)(2,1)} %param.11) | data formatting | bytes 4096 | tf_op jit(solution)/shard_map/reshape | solution.py:418
  1.3 2.2 %copy.7.tokens = bf16[22,11,1024]{2,1,0:T(8,128)(2,1)} copy(bf16[22,11,1024]{2,0,1:T(8,128)(2,1)} %param.6) | data formatting | bytes 991232 | tf_op args[0]
  3.5 2.6 %copy.8.wq_in = bf16[2,1024,320]{2,1,0:T(8,128)(2,1)} copy(bf16[2,1024,320]{1,2,0:T(8,128)(2,1)} %param.7) | data formatting | bytes 2621440 | tf_op args[1]
  6.0 102.3 %shard_map.64 = bf16[22,11,1024]{2,1,0:T(8,128)(2,1)} custom-call(bf16[22,11,1024]{2,1,0:T(8,128)(2,1)} %copy.7.tokens, bf16[2,1024,320]{2,1,0:T(8,128)(2,1)} %copy.8.wq_in, bf16[2,1024,256]{2,1,0:T(8,128)(2,1)} %wo_in.1, f32[2,1024]{1,0:T(2,128)} %gain.1, bf16[9,1024]{1,0:T(8,128)(2,1)} %conv_w.1, bf16[1,1024]{1,0:T(2,128)(2,1)} %reshape.3.conv_b), custom_call_target="tpu_custom_call" | custom-call | tf_op jit(solution)/shard_map/pallas_call | solution.py:385
  108.4 2.2 %copy.9 = bf16[22,11,1024]{2,0,1:T(8,128)(2,1)} copy(bf16[22,11,1024]{2,1,0:T(8,128)(2,1)} %shard_map.64) | data formatting | bytes 991232 | tf_op jit(solution)/shard_map/pallas_call | solution.py:385

commit v2 on v1

v2 whole, which is shorter than its diff:
```python
import functools

import jax
import jax.numpy as jnp
from jax import lax
from jax.experimental import pallas as pl
from jax.experimental.pallas import tpu as pltpu
from jax.sharding import PartitionSpec as P

HEADS = 16
KV = 2
HD = 64


def with_halo(cells, sides, width, closed):
    for axis, dim in sides:
        count = lax.axis_size(axis)
        ends = count if closed else count - 1
        head = lax.slice_in_dim(cells, 0, width, axis=dim)
        tail = lax.slice_in_dim(cells, cells.shape[dim] - width, cells.shape[dim], axis=dim)
        cells = jnp.concatenate(
            [
                lax.ppermute(tail, axis, [(i, (i + 1) % count) for i in range(ends)]),
                cells,
                lax.ppermute(head, axis, [((i + 1) % count, i) for i in range(ends)]),
            ],
            axis=dim,
        )
    return cells


def split_keyval(keyval):
    batch, length, columns = keyval.shape
    keys = keyval[..., : KV * HD].reshape(batch, length, KV, HD)
    values = keyval[..., KV * HD :].reshape(batch, length, KV, HD)
    return (keys, values)


def line_scores(query, keys):
    batch, length, feature = query.shape
    grouped = query.reshape(batch, length, KV, HEADS // KV, HD)
    return jnp.einsum(
        "nqgjd,nkgd->ngjqk", grouped, keys, preferred_element_type=jnp.float32
    ) * HD ** (-0.5)


def attend_lines(query, keyval):
    batch, length, feature = query.shape
    keys, values = split_keyval(keyval)
    scores = line_scores(query, keys)
    peak = jnp.max(scores, axis=-1, keepdims=True)
    expon = jnp.exp(scores - peak)
    denominator = jnp.sum(expon, axis=-1)
    mixed = jnp.einsum(
        "ngjqk,nkgd->nqgjd", expon.astype(jnp.bfloat16), values, preferred_element_type=jnp.float32
    )
    mixed = mixed / jnp.transpose(denominator, (0, 3, 1, 2))[..., None]
    return mixed.reshape(batch, length, feature).astype(jnp.bfloat16)


def rms_norm(current, gain):
    values = current.astype(jnp.float32)
    scaled = values * lax.rsqrt(jnp.mean(values * values, axis=-1, keepdims=True) + 1e-06)
    return (scaled * gain).astype(jnp.bfloat16)


def shards(tokens, qkv_weight, out_weight, norm_gain, conv_weight, conv_bias):
    lat_rows, lon_cols, feature = tokens.shape
    widened = with_halo(tokens, (("lon", 1),), 1, True)
    padded = with_halo(widened, (("lat", 0),), 1, False)
    total = tokens.astype(jnp.float32) + conv_bias.astype(jnp.float32)
    for shift_lat in range(3):
        for shift_lon in range(3):
            window = padded[
                shift_lat : shift_lat + lat_rows, shift_lon : shift_lon + lon_cols
            ].astype(jnp.float32)
            total = total + conv_weight[3 * shift_lat + shift_lon].astype(jnp.float32) * window
    current = total.astype(jnp.bfloat16)
    for section_index in range(2):
        weight_in, weight_out = (
            lax.all_gather(qkv_weight[section_index], "lon", axis=1, tiled=True),
            lax.all_gather(out_weight[section_index], "lon", axis=1, tiled=True),
        )
        normed = rms_norm(current, norm_gain[section_index])
        projected = jnp.dot(
            normed.reshape(-1, feature), weight_in, preferred_element_type=jnp.float32
        )
        projected = projected.astype(jnp.bfloat16).reshape(lat_rows, lon_cols, -1)
        query = projected[..., :feature]
        keyval = projected[..., feature:]
        if section_index == 0:
            gathered = lax.all_gather(keyval, "lon", axis=1, tiled=True)
            attended = attend_lines(query, gathered)
        else:
            gathered = lax.all_gather(keyval, "lat", axis=0, tiled=True)
            attended = attend_lines(
                jnp.transpose(query, (1, 0, 2)), jnp.transpose(gathered, (1, 0, 2))
            )
            attended = jnp.transpose(attended, (1, 0, 2))
        output = jnp.dot(
            attended.reshape(-1, feature), weight_out, preferred_element_type=jnp.float32
        )
        current = (
            current.astype(jnp.float32) + output.reshape(lat_rows, lon_cols, feature)
        ).astype(jnp.bfloat16)
    return current


MESH = pl.DeviceIdType.MESH
F32 = jnp.float32
BF16 = jnp.bfloat16
PLANE = 8
UNROLL = 1


def remote(src, dst, send, recv, device):
    return pltpu.make_async_remote_copy(
        src_ref=src, dst_ref=dst, send_sem=send, recv_sem=recv, device_id=device, device_id_type=MESH
    )


def step_kernel(
    nlat, nlon, tokens, wq_in, wo_in, gain, conv_w, conv_b, out,
    wq, wo, pad, edgef, edge, hcol, hrow, hcor, cur, normed, turned, turn, proj, att, kvs, kv0, kv1, kvt,
    sem_w, sem_z, sem_f, sem_c, sem_hs, sem_hr, sem_ks, sem_kr, sem_l,
):
    cols, rows, feature = tokens.shape
    step0, step1, sent = 16, 32, 24
    count = rows * step0
    ens, lat, lon = lax.axis_index("ens"), lax.axis_index("lat"), lax.axis_index("lon")
    here = ens * 4 + lax.rem(lat, 4)

    def flip(value, bit):
        return value + bit - 2 * bit * lax.rem(value // bit, 2)

    wide = wq_in.shape[1]
    piece_q, piece_o = wide // PLANE, feature // PLANE
    dev_core = (ens, flip(lat, 1), lon)
    dev_x = (ens, flip(lat, 2), lon)
    dev_y = (1 - ens, lat, lon)
    dev_xy = (1 - ens, flip(lat, 2), lon)
    p_core, p_x, p_y = flip(here, 1), flip(here, 2), flip(here, 4)
    p_xy = flip(p_x, 4)
    far = [lax.rem(lon + d, nlon) for d in range(nlon)]
    farlat = [lax.rem(lat + d, nlat) for d in range(nlat)]

    def rows_of(m, p):
        size = piece_o if m % 2 else piece_q
        return pl.ds(pl.multiple_of(p * size, size), size)

    def part(m, s, p):
        return (wo if m % 2 else wq).at[m // 2, s, rows_of(m, p), :]

    def own(m):
        return (wo_in if m % 2 else wq_in).at[m // 2]

    cur[...] = jnp.zeros_like(cur)
    normed[...] = jnp.zeros_like(normed)
    kv0[...] = jnp.zeros_like(kv0)
    kv1[...] = jnp.zeros_like(kv1)

    barrier = pltpu.get_barrier_semaphore()
    greet = [(ens, lat, far[d]) for d in range(1, nlon)]
    greet += [(ens, farlat[d], lon) for d in range(1, nlat)]
    greet += [(ens, farlat[a], far[b]) for a in (1, nlat - 1) for b in (1, nlon - 1)]
    greet += [dev_y, dev_xy]
    for device in greet:
        pl.semaphore_signal(barrier, inc=1, device_id=device, device_id_type=MESH)
    pl.semaphore_wait(barrier, len(greet))

    pending, kv_sends = [], []

    def launch(copy):
        copy.start()
        pending.append(copy)

    def send_z(m):
        for d in range(1, nlon):
            launch(remote(
                own(m).at[rows_of(m, here), :],
                part(m, lon, here), sem_z.at[m, d], sem_w.at[m, lon, here], (ens, lat, far[d]),
            ))

    def arrived(m, s, p):
        remote(part(m, s, p), part(m, s, p), sem_z.at[m, 0], sem_w.at[m, s, p], dev_core).wait_recv()

    def pass_on(m, s, p, send, device):
        launch(remote(part(m, s, p), part(m, s, p), send, sem_w.at[m, s, p], device))

    def spread(m):
        for d in (1, 3, 2) if nlon == 4 else range(1, nlon):
            arrived(m, far[d], here)
            pass_on(m, far[d], here, sem_f.at[m, d, 0], dev_x)
            pass_on(m, far[d], here, sem_f.at[m, d, 1], dev_y)
            pass_on(m, far[d], here, sem_f.at[m, d, 3], dev_core)

    def share(m):
        for d in (1, 3, 2) if nlon == 4 else range(1, nlon):
            for k, (p, onward) in enumerate(((p_x, dev_y), (p_y, dev_x))):
                arrived(m, far[d], p)
                if (m + d) % 2 == k:
                    pass_on(m, far[d], p, sem_f.at[m, d, 2], onward)
                pass_on(m, far[d], p, sem_c.at[m, d, k], dev_core)

    def share_diagonal(m):
        for d in (1, 3, 2) if nlon == 4 else range(1, nlon):
            arrived(m, far[d], p_xy)
            pass_on(m, far[d], p_xy, sem_c.at[m, d, 2], dev_core)

    def finish(m):
        pltpu.make_async_copy(own(m), (wo if m % 2 else wq).at[m // 2, lon], sem_l.at[m]).wait()
        for d in range(1, nlon):
            for p in (p_core, flip(p_x, 1), flip(p_y, 1), flip(p_xy, 1)):
                arrived(m, far[d], p)

    send_z(0)
    for m in range(4):
        pltpu.make_async_copy(own(m), (wo if m % 2 else wq).at[m // 2, lon], sem_l.at[m]).start()

    edgef[...] = jnp.zeros_like(edgef)
    for j in range(cols):
        line = tokens[j].astype(F32)
        pad[1 + j, 8 : 8 + rows, :] = line
        edgef[0, j : j + 1, :] = line[0:1]
        edgef[1, j : j + 1, :] = line[rows - 1 : rows]
    edge[...] = edgef[...].astype(BF16)
    north, south, west, east = farlat[nlat - 1], farlat[1], far[nlon - 1], far[1]
    halos = [
        (tokens.at[cols - 1], hcol.at[0], (ens, lat, east)),
        (tokens.at[0], hcol.at[1], (ens, lat, west)),
        (edge.at[1], hrow.at[0], (ens, south, lon)),
        (edge.at[0], hrow.at[1], (ens, north, lon)),
        (edge.at[1], hcor.at[0], (ens, south, east)),
        (edge.at[1], hcor.at[1], (ens, south, west)),
        (edge.at[0], hcor.at[2], (ens, north, east)),
        (edge.at[0], hcor.at[3], (ens, north, west)),
    ]
    hcopies = [remote(a, b, sem_hs.at[k], sem_hr.at[k], dev) for k, (a, b, dev) in enumerate(halos)]
    for copy in hcopies:
        launch(copy)
    for m in (1, 2, 3):
        send_z(m)
    spread(0)
    for copy in hcopies:
        copy.wait_recv()

    for side, place in ((0, 0), (1, 1 + cols)):
        pad[place, 8 : 8 + rows, :] = hcol[side].astype(F32)
    for k, (spot, inside) in enumerate(((7, lat > 0), (8 + rows, lat < nlat - 1))):
        keep = jnp.where(inside, 1.0, 0.0).astype(F32)
        line = hrow[k].astype(F32) * keep
        for j in range(cols):
            pad[1 + j, spot : spot + 1, :] = line[j : j + 1]
        pad[0, spot : spot + 1, :] = hcor[2 * k].astype(F32)[cols - 1 : cols] * keep
        pad[1 + cols, spot : spot + 1, :] = hcor[2 * k + 1].astype(F32)[0:1] * keep

    taps = conv_w[...].astype(F32)
    bias = conv_b[...].astype(F32).reshape(1, feature)
    alive = lax.broadcasted_iota(jnp.int32, (sent, 1), 0) < rows

    def rms(values, k):
        scaled = values * lax.rsqrt(jnp.mean(values * values, axis=-1, keepdims=True) + 1e-06)
        return (scaled * gain[k : k + 1, :]).astype(BF16)

    def conv_line(j, carry):
        total = pad[j + 1, 8 : 8 + sent, :] + bias
        for a in range(3):
            for b in range(3):
                total = total + taps[3 * a + b : 3 * a + b + 1] * pad[j + b, 7 + a : 7 + a + sent, :]
        total = jnp.where(alive, total, 0.0)
        rounded = jnp.concatenate([total, jnp.zeros((step1 - sent, feature), F32)], axis=0).astype(BF16)
        spot = pl.ds(pl.multiple_of(j * step1, step1), step1)
        cur[spot, :] = rounded
        normed[spot, :] = rms(rounded.astype(F32), 0)
        return carry

    lax.fori_loop(0, cols, conv_line, 0)
    to = lax.broadcasted_iota(jnp.int32, (count, count), 0)
    fro = lax.broadcasted_iota(jnp.int32, (count, count), 1)
    turn[0] = jnp.where(
        (fro == lax.rem(to, step0) * step1 + to // step0) & (lax.rem(to, step0) < cols), 1.0, 0.0
    ).astype(BF16)
    turn[1] = jnp.where(
        (fro == lax.rem(to, step1) * step0 + to // step1) & (lax.rem(to, step1) < rows), 1.0, 0.0
    ).astype(BF16)

    def halves(block):
        left = lax.broadcasted_iota(jnp.int32, block.shape, 1) < HD
        swapped = jnp.concatenate([block[:, HD:], block[:, :HD]], axis=1)
        zero = jnp.zeros_like(block)
        first = (jnp.where(left, block, zero), jnp.where(left, zero, swapped))
        second = (jnp.where(left, swapped, zero), jnp.where(left, zero, block))
        return (first, second)

    def attend(keys_of, values_of, width, blocks, step, valid):
        pairs = HEADS // KV // 2
        packed = 2 * width <= 128

        def contract(a, b):
            return lax.dot_general(a, b, (((1,), (1,)), ((), ())), preferred_element_type=F32)

        def body(r, carry):
            spot = pl.ds(pl.multiple_of(r * step, step), step)
            kh, vh = halves(keys_of(spot)), halves(values_of(spot))
            sides = lax.broadcasted_iota(jnp.int32, (width, 2 * HD), 1) < HD
            ones = [jnp.where(sides, 1.0, 0.0).astype(BF16), jnp.where(sides, 0.0, 1.0).astype(BF16)]
            span = 2 * width if packed else width
            lane = lax.broadcasted_iota(jnp.int32, (1, span), 1)
            valid_key = lax.rem(lane, step) < valid
            for g in range(KV):
                base = g * pairs
                query = jnp.concatenate(
                    [proj[spot, (base + p) * 128 : (base + p + 1) * 128] for p in range(pairs)], axis=0
                )
                blend = [jnp.concatenate([vh[g][half], ones[half]], axis=1) for half in range(2)]
                if packed:
                    scores = contract(query, jnp.concatenate(kh[g], axis=0))
                    near = jnp.where(valid_key & (lane < width), scores, -jnp.inf)
                    away = jnp.where(valid_key & (lane >= width), scores, -jnp.inf)
                    peak = jnp.where(
                        lane < width,
                        jnp.max(near, axis=-1, keepdims=True),
                        jnp.max(away, axis=-1, keepdims=True),
                    )
                    expon = jnp.where(valid_key, jnp.exp(jnp.where(valid_key, scores - peak, 0.0)), 0.0)
                    both = jnp.dot(
                        expon.astype(BF16), jnp.concatenate(blend, axis=0), preferred_element_type=F32
                    )
                else:
                    both = None
                    for half in range(2):
                        scores = jnp.where(valid_key, contract(query, kh[g][half]), -jnp.inf)
                        expon = jnp.exp(scores - jnp.max(scores, axis=-1, keepdims=True))
                        term = jnp.dot(expon.astype(BF16), blend[half], preferred_element_type=F32)
                        both = term if both is None else both + term
                mixed = (both[:, : 2 * HD] / both[:, 2 * HD :]).astype(BF16)
                for p in range(pairs):
                    att[spot, (base + p) * 128 : (base + p + 1) * 128] = mixed[p * step : (p + 1) * step]
            return carry

        lax.fori_loop(0, blocks, body, 0, unroll=UNROLL)

    def wide_rows(k, low, high):
        return wq.at[k].reshape(nlon * wide, feature)[low:high, :]

    def many(a, b):
        return lax.dot_general(a, b, (((1,), (1,)), ((), ())), preferred_element_type=F32)

    def query_of(k, source):
        for t in range(0, feature, 256):
            proj[:, t : t + 256] = (many(source[...], wide_rows(k, t, t + 256)) * HD ** (-0.5)).astype(BF16)

    def send_kv(k, kv, targets, mine):
        for copy in kv_sends:
            copy.wait_send()
        kv_sends.clear()
        fresh = many(normed[...], wide_rows(k, feature, feature + 2 * KV * HD)).astype(BF16)
        kvs[...] = fresh.reshape(cols, step1, 2 * KV * HD)
        for d, device in targets:
            copy = remote(
                kvs.at[:, pl.ds(0, sent), :], kv.at[mine, :, pl.ds(0, sent), :],
                sem_ks.at[k, d], sem_kr.at[k, mine], device,
            )
            copy.start()
            kv_sends.append(copy)

    def take_kv(k, kv, sources):
        for s in sources:
            spot = kv.at[s, :, pl.ds(0, sent), :]
            remote(spot, spot, sem_ks.at[k, 0], sem_kr.at[k, s], dev_core).wait_recv()

    def back(k, values, s, width):
        lanes = pl.ds(s * width, width)
        return (cur[:, lanes].astype(F32) + jnp.dot(values, wo[k, s], preferred_element_type=F32)).astype(BF16)

    share(0)
    spread(1)
    share_diagonal(0)
    turned[...] = jnp.dot(turn[0], normed[...], preferred_element_type=F32).astype(BF16)
    share(1)
    finish(0)
    send_kv(0, kv0, [(d, (ens, lat, far[d])) for d in range(1, nlon)], lon)
    query_of(0, turned)
    share_diagonal(1)
    spread(2)
    take_kv(0, kv0, far[1:])
    flat = (count, 2 * KV * HD)
    kv0[lon] = kvs[...]
    for s in range(nlon):
        kvt[s] = jnp.dot(turn[0], kv0[s].reshape(flat), preferred_element_type=F32).astype(BF16)

    def gathered(buffer, parts, low, high):
        return lambda spot: jnp.concatenate([buffer[s, spot, low:high] for s in range(parts)], axis=0)

    def lined(low, high):
        def read(spot):
            j = spot.start // step1
            return jnp.concatenate([kv1[s, j, :, low:high] for s in range(nlat)], axis=0)

        return read

    share(2)
    attend(
        gathered(kvt, nlon, 0, KV * HD), gathered(kvt, nlon, KV * HD, 2 * KV * HD),
        nlon * step0, rows, step0, cols,
    )
    share_diagonal(2)
    spread(3)
    turned[...] = jnp.dot(turn[1], att[...], preferred_element_type=F32).astype(BF16)
    finish(1)
    width = wo.shape[3]
    for s in range(nlon):
        cur[:, s * width : (s + 1) * width] = back(0, turned[...], s, width)

    def norm_row(i, carry):
        spot = pl.ds(pl.multiple_of(i * step1, step1), step1)
        normed[spot, :] = rms(cur[spot, :].astype(F32), 1)
        return carry

    lax.fori_loop(0, count // step1, norm_row, 0)
    finish(2)
    send_kv(1, kv1, [(d, (ens, farlat[d], lon)) for d in range(1, nlat)], lat)
    share(3)
    query_of(1, normed)
    share_diagonal(3)
    take_kv(1, kv1, farlat[1:])
    kv1[lat] = kvs[...]
    attend(lined(0, KV * HD), lined(KV * HD, 2 * KV * HD), nlat * step1, cols, step1, rows)
    finish(3)
    for s in range(nlon):
        done = back(1, att[...], s, width)
        out[:, :, s * width : (s + 1) * width] = done.reshape(cols, step1, width)[:, :rows, :]
    for copy in pending + kv_sends:
        copy.wait_send()


def fused(tokens, qkv_weight, out_weight, norm_gain, conv_weight, conv_bias, nlat, nlon):
    tokens, qkv_weight = jnp.swapaxes(tokens, 0, 1), jnp.swapaxes(qkv_weight, 1, 2)
    cols, rows, feature = tokens.shape
    count = rows * 16
    columns = 2 * KV * HD
    vmem = pl.BlockSpec(memory_space=pltpu.VMEM)
    hbm = pl.BlockSpec(memory_space=pl.ANY)
    dma = pltpu.SemaphoreType.DMA
    result = pl.pallas_call(
        functools.partial(step_kernel, nlat, nlon),
        out_shape=jax.ShapeDtypeStruct(tokens.shape, BF16),
        in_specs=[vmem, hbm, hbm, vmem, vmem, vmem],
        out_specs=vmem,
        scratch_shapes=[
            pltpu.VMEM((2, nlon) + qkv_weight.shape[1:], BF16),
            pltpu.VMEM((2, nlon) + out_weight.shape[1:], BF16),
            pltpu.VMEM((cols + 2, 40, feature), F32),
            pltpu.VMEM((2, 16, feature), F32),
            pltpu.VMEM((2, 16, feature), BF16),
            pltpu.VMEM((2, rows, feature), BF16),
            pltpu.VMEM((2, 16, feature), BF16),
            pltpu.VMEM((4, 16, feature), BF16),
            pltpu.VMEM((count, feature), BF16),
            pltpu.VMEM((count, feature), BF16),
            pltpu.VMEM((count, feature), BF16),
            pltpu.VMEM((2, count, count), BF16),
            pltpu.VMEM((count, feature), BF16),
            pltpu.VMEM((count, feature), BF16),
            pltpu.VMEM((cols, 32, columns), BF16),
            pltpu.VMEM((nlon, cols, 32, columns), BF16),
            pltpu.VMEM((nlat, cols, 32, columns), BF16),
            pltpu.VMEM((nlon, count, columns), BF16),
            dma((4, nlon, PLANE)),
            dma((4, nlon)),
            dma((4, nlon, 4)),
            dma((4, nlon, 3)),
            dma((8,)),
            dma((8,)),
            dma((2, max(nlat, nlon))),
            dma((2, max(nlat, nlon))),
            dma((4,)),
        ],
        compiler_params=pltpu.CompilerParams(
            collective_id=0, has_side_effects=True, vmem_limit_bytes=56 * 2**20
        ),
    )(tokens, qkv_weight, out_weight, norm_gain, conv_weight, conv_bias)
    return jnp.swapaxes(result, 0, 1)


def entry(tokens, qkv_weight, out_weight, norm_gain, conv_weight, conv_bias):
    nens, nlat, nlon = (lax.axis_size(name) for name in ("ens", "lat", "lon"))
    if (nens, nlat, nlon) == (2, 4, 4) and tokens.shape[:2] == (22, 11):
        return fused(
            tokens, qkv_weight, out_weight, norm_gain, conv_weight, conv_bias, nlat, nlon
        )
    return shards(tokens, qkv_weight, out_weight, norm_gain, conv_weight, conv_bias)


def solution(mesh):
    in_specs = (
        P(("ens", "lat"), "lon", None),
        P(None, None, "lon"),
        P(None, None, "lon"),
        P(),
        P(),
        P(),
    )
    out_specs = P(("ens", "lat"), "lon", None)
    return jax.shard_map(entry, mesh=mesh, in_specs=in_specs, out_specs=out_specs, check_vma=False)
```

time: 111 us -> 90 us (0.81)
  Pallas kernels: 102 us -> 87.6 us
  local copies, waits for them, and re-layouts: 8.25 us -> 1.88 us
    pallas_call x1, Pallas kernels: 102 us -> 87.6 us  [fused(): pl.pallas_call(functools.partial(step_kernel, nlat, nlon), out_shape=jax....]
    unnamed x2 -> x1, local copies, waits for them, and re-layouts: 4.76 us -> 1.88 us
    pallas_call x1 -> x0, local copies, waits for them, and re-layouts: 2.21 us -> none  [fused(): pl.pallas_call(functools.partial(step_kernel, nlat, nlon), out_shape=jax....]
    reshape x1 -> x0, local copies, waits for them, and re-layouts: 1.28 us -> none  [fused(): conv_bias.reshape(1, feature)]
where the time goes in v2:
time: 90 us; the launch traced here: 89.5 us
  Pallas kernels  87.6 us (97%)
  local copies, waits for them, and re-layouts  1.88 us (2%)
    pallas_call x1, Pallas kernels, fused(): pl.pallas_call(functools.partial(step_kernel, nlat, nlon), out_shape=jax....  87.6 us
    unnamed x1, local copies, waits for them, and re-layouts  1.88 us

profile of v2, /device:TPU:13, one launch (start us, length us, event | category | flops | bytes accessed | tf_op | source)
XLA Modules:
  0.0 89.5 jit_solution(667839713021589295)
XLA Ops:
  0.0 87.6 %shard_map.64 = bf16[11,22,1024]{2,1,0:T(8,128)(2,1)} custom-call(bf16[11,22,1024]{2,1,0:T(8,128)(2,1)} %bitcast.5, bf16[2,320,1024]{2,1,0:T(8,128)(2,1)} %bitcast.4, bf16[2,1024,256]{2,1,0:T(8,128)(2,1)} %wo_in.1, f32[2,1024]{1,0:T(2,128)} %gain.1, bf16[9,1024]{1,0:T(8,128)(2,1)} %conv_w.1, bf16[1024]{0:T(1024)(128)(2,1)} %conv_b.1), custom_call_target="tpu_custom_call" | custom-call | tf_op jit(solution)/shard_map/pallas_call | solution.py:445
  87.6 1.9 %copy.8 = bf16[22,11,1024]{2,0,1:T(8,128)(2,1)} copy(bf16[22,11,1024]{2,0,1:T(8,128)(2,1)} %bitcast.3) | data formatting | bytes 991232

commit v3 on v2

--- a/solution.py
+++ b/solution.py
@@ -110,7 +110,8 @@
 F32 = jnp.float32
 BF16 = jnp.bfloat16
 PLANE = 8
-UNROLL = 1
+UNROLL0 = 11
+UNROLL1 = 11
 
 
 def remote(src, dst, send, recv, device):
@@ -168,7 +169,7 @@
         pl.semaphore_signal(barrier, inc=1, device_id=device, device_id_type=MESH)
     pl.semaphore_wait(barrier, len(greet))
 
-    pending, kv_sends = [], []
+    pending, kv_sends = [], [[] for g in range(KV)]
 
     def launch(copy):
         copy.start()
@@ -275,24 +276,24 @@
         return carry
 
     lax.fori_loop(0, cols, conv_line, 0)
-    to = lax.broadcasted_iota(jnp.int32, (count, count), 0)
+    to = lax.broadcasted_iota(jnp.int32, (count, 1), 0)
     fro = lax.broadcasted_iota(jnp.int32, (count, count), 1)
     turn[0] = jnp.where(
-        (fro == lax.rem(to, step0) * step1 + to // step0) & (lax.rem(to, step0) < cols), 1.0, 0.0
+        fro == jnp.where(lax.rem(to, step0) < cols, lax.rem(to, step0) * step1 + to // step0, -1), 1.0, 0.0
     ).astype(BF16)
     turn[1] = jnp.where(
-        (fro == lax.rem(to, step1) * step0 + to // step1) & (lax.rem(to, step1) < rows), 1.0, 0.0
+        fro == jnp.where(lax.rem(to, step1) < rows, lax.rem(to, step1) * step0 + to // step1, -1), 1.0, 0.0
     ).astype(BF16)
 
     def halves(block):
         left = lax.broadcasted_iota(jnp.int32, block.shape, 1) < HD
         swapped = jnp.concatenate([block[:, HD:], block[:, :HD]], axis=1)
         zero = jnp.zeros_like(block)
-        first = (jnp.where(left, block, zero), jnp.where(left, zero, swapped))
-        second = (jnp.where(left, swapped, zero), jnp.where(left, zero, block))
-        return (first, second)
-
-    def attend(keys_of, values_of, width, blocks, step, valid):
+        keys = (jnp.where(left, block, zero), jnp.where(left, zero, swapped))
+        values = (jnp.where(left, swapped, zero), jnp.where(left, zero, block))
+        return keys, values
+
+    def attend(g, block_of, width, blocks, step, valid):
         pairs = HEADS // KV // 2
         packed = 2 * width <= 128
 
@@ -301,44 +302,43 @@
 
         def body(r, carry):
             spot = pl.ds(pl.multiple_of(r * step, step), step)
-            kh, vh = halves(keys_of(spot)), halves(values_of(spot))
+            kh, vh = halves(block_of(spot))
             sides = lax.broadcasted_iota(jnp.int32, (width, 2 * HD), 1) < HD
             ones = [jnp.where(sides, 1.0, 0.0).astype(BF16), jnp.where(sides, 0.0, 1.0).astype(BF16)]
             span = 2 * width if packed else width
             lane = lax.broadcasted_iota(jnp.int32, (1, span), 1)
             valid_key = lax.rem(lane, step) < valid
-            for g in range(KV):
-                base = g * pairs
-                query = jnp.concatenate(
-                    [proj[spot, (base + p) * 128 : (base + p + 1) * 128] for p in range(pairs)], axis=0
+            base = g * pairs
+            query = jnp.concatenate(
+                [proj[spot, (base + p) * 128 : (base + p + 1) * 128] for p in range(pairs)], axis=0
+            )
+            blend = [jnp.concatenate([vh[half], ones[half]], axis=1) for half in range(2)]
+            if packed:
+                scores = contract(query, jnp.concatenate(kh, axis=0))
+                near = jnp.where(valid_key & (lane < width), scores, -jnp.inf)
+                away = jnp.where(valid_key & (lane >= width), scores, -jnp.inf)
+                peak = jnp.where(
+                    lane < width,
+                    jnp.max(near, axis=-1, keepdims=True),
+                    jnp.max(away, axis=-1, keepdims=True),
                 )
-                blend = [jnp.concatenate([vh[g][half], ones[half]], axis=1) for half in range(2)]
-                if packed:
-                    scores = contract(query, jnp.concatenate(kh[g], axis=0))
-                    near = jnp.where(valid_key & (lane < width), scores, -jnp.inf)
-                    away = jnp.where(valid_key & (lane >= width), scores, -jnp.inf)
-                    peak = jnp.where(
-                        lane < width,
-                        jnp.max(near, axis=-1, keepdims=True),
-                        jnp.max(away, axis=-1, keepdims=True),
-                    )
-                    expon = jnp.where(valid_key, jnp.exp(jnp.where(valid_key, scores - peak, 0.0)), 0.0)
-                    both = jnp.dot(
-                        expon.astype(BF16), jnp.concatenate(blend, axis=0), preferred_element_type=F32
-                    )
-                else:
-                    both = None
-                    for half in range(2):
-                        scores = jnp.where(valid_key, contract(query, kh[g][half]), -jnp.inf)
-                        expon = jnp.exp(scores - jnp.max(scores, axis=-1, keepdims=True))
-                        term = jnp.dot(expon.astype(BF16), blend[half], preferred_element_type=F32)
-                        both = term if both is None else both + term
-                mixed = (both[:, : 2 * HD] / both[:, 2 * HD :]).astype(BF16)
-                for p in range(pairs):
-                    att[spot, (base + p) * 128 : (base + p + 1) * 128] = mixed[p * step : (p + 1) * step]
+                expon = jnp.where(valid_key, jnp.exp(jnp.where(valid_key, scores - peak, 0.0)), 0.0)
+                both = jnp.dot(
+                    expon.astype(BF16), jnp.concatenate(blend, axis=0), preferred_element_type=F32
+                )
+            else:
+                both = None
+                for half in range(2):
+                    scores = jnp.where(valid_key, contract(query, kh[half]), -jnp.inf)
+                    expon = jnp.exp(scores - jnp.max(scores, axis=-1, keepdims=True))
+                    term = jnp.dot(expon.astype(BF16), blend[half], preferred_element_type=F32)
+                    both = term if both is None else both + term
+            mixed = (both[:, : 2 * HD] / both[:, 2 * HD :]).astype(BF16)
+            for p in range(pairs):
+                att[spot, (base + p) * 128 : (base + p + 1) * 128] = mixed[p * step : (p + 1) * step]
             return carry
 
-        lax.fori_loop(0, blocks, body, 0, unroll=UNROLL)
+        lax.fori_loop(0, blocks, body, 0, unroll=UNROLL0 if packed else UNROLL1)
 
     def wide_rows(k, low, high):
         return wq.at[k].reshape(nlon * wide, feature)[low:high, :]
@@ -350,64 +350,69 @@
         for t in range(0, feature, 256):
             proj[:, t : t + 256] = (many(source[...], wide_rows(k, t, t + 256)) * HD ** (-0.5)).astype(BF16)
 
-    def send_kv(k, kv, targets, mine):
-        for copy in kv_sends:
+    def send_kv(k, g, kv, targets, mine):
+        for copy in kv_sends[g]:
             copy.wait_send()
-        kv_sends.clear()
-        fresh = many(normed[...], wide_rows(k, feature, feature + 2 * KV * HD)).astype(BF16)
-        kvs[...] = fresh.reshape(cols, step1, 2 * KV * HD)
+        kv_sends[g].clear()
+        low = feature + g * HD
+        both = jnp.concatenate(
+            [wide_rows(k, low, low + HD), wide_rows(k, low + KV * HD, low + KV * HD + HD)], axis=0
+        )
+        kvs[g] = many(normed[...], both).astype(BF16).reshape(cols, step1, 2 * HD)
         for d, device in targets:
             copy = remote(
-                kvs.at[:, pl.ds(0, sent), :], kv.at[mine, :, pl.ds(0, sent), :],
-                sem_ks.at[k, d], sem_kr.at[k, mine], device,
+                kvs.at[g, :, pl.ds(0, sent), :], kv.at[g, mine, :, pl.ds(0, sent), :],
+                sem_ks.at[k, g, d], sem_kr.at[k, g, mine], device,
             )
             copy.start()
-            kv_sends.append(copy)
-
-    def take_kv(k, kv, sources):
+            kv_sends[g].append(copy)
+        kv[g, mine] = kvs[g]
+
+    def take_kv(k, g, kv, sources):
         for s in sources:
-            spot = kv.at[s, :, pl.ds(0, sent), :]
-            remote(spot, spot, sem_ks.at[k, 0], sem_kr.at[k, s], dev_core).wait_recv()
+            spot = kv.at[g, s, :, pl.ds(0, sent), :]
+            remote(spot, spot, sem_ks.at[k, g, 0], sem_kr.at[k, g, s], dev_core).wait_recv()
 
     def back(k, values, s, width):
         lanes = pl.ds(s * width, width)
         return (cur[:, lanes].astype(F32) + jnp.dot(values, wo[k, s], preferred_element_type=F32)).astype(BF16)
 
+    turned[...] = jnp.dot(turn[0], normed[...], preferred_element_type=F32).astype(BF16)
     share(0)
     spread(1)
     share_diagonal(0)
-    turned[...] = jnp.dot(turn[0], normed[...], preferred_element_type=F32).astype(BF16)
+    finish(0)
+    for g in range(KV):
+        send_kv(0, g, kv0, [(d, (ens, lat, far[d])) for d in range(1, nlon)], lon)
+    spread(2)
+    query_of(0, turned)
     share(1)
-    finish(0)
-    send_kv(0, kv0, [(d, (ens, lat, far[d])) for d in range(1, nlon)], lon)
-    query_of(0, turned)
-    share_diagonal(1)
-    spread(2)
-    take_kv(0, kv0, far[1:])
-    flat = (count, 2 * KV * HD)
-    kv0[lon] = kvs[...]
-    for s in range(nlon):
-        kvt[s] = jnp.dot(turn[0], kv0[s].reshape(flat), preferred_element_type=F32).astype(BF16)
-
-    def gathered(buffer, parts, low, high):
-        return lambda spot: jnp.concatenate([buffer[s, spot, low:high] for s in range(parts)], axis=0)
-
-    def lined(low, high):
+
+    def gathered(g):
+        return lambda spot: jnp.concatenate([kvt[g, s, spot, :] for s in range(nlon)], axis=0)
+
+    def lined(g):
         def read(spot):
             j = spot.start // step1
-            return jnp.concatenate([kv1[s, j, :, low:high] for s in range(nlat)], axis=0)
+            return jnp.concatenate([kv1[g, s, j] for s in range(nlat)], axis=0)
 
         return read
 
-    share(2)
-    attend(
-        gathered(kvt, nlon, 0, KV * HD), gathered(kvt, nlon, KV * HD, 2 * KV * HD),
-        nlon * step0, rows, step0, cols,
-    )
-    share_diagonal(2)
-    spread(3)
+    for g in range(KV):
+        take_kv(0, g, kv0, far[1:])
+        for s in range(nlon):
+            kvt[g, s] = jnp.dot(
+                turn[0], kv0[g, s].reshape(count, 2 * HD), preferred_element_type=F32
+            ).astype(BF16)
+        attend(g, gathered(g), nlon * step0, rows, step0, cols)
+        if g == 0:
+            share_diagonal(1)
+            share(2)
+            spread(3)
     turned[...] = jnp.dot(turn[1], att[...], preferred_element_type=F32).astype(BF16)
     finish(1)
+    share_diagonal(2)
+    share(3)
     width = wo.shape[3]
     for s in range(nlon):
         cur[:, s * width : (s + 1) * width] = back(0, turned[...], s, width)
@@ -419,18 +424,18 @@
 
     lax.fori_loop(0, count // step1, norm_row, 0)
     finish(2)
-    send_kv(1, kv1, [(d, (ens, farlat[d], lon)) for d in range(1, nlat)], lat)
-    share(3)
+    for g in range(KV):
+        send_kv(1, g, kv1, [(d, (ens, farlat[d], lon)) for d in range(1, nlat)], lat)
     query_of(1, normed)
     share_diagonal(3)
-    take_kv(1, kv1, farlat[1:])
-    kv1[lat] = kvs[...]
-    attend(lined(0, KV * HD), lined(KV * HD, 2 * KV * HD), nlat * step1, cols, step1, rows)
+    for g in range(KV):
+        take_kv(1, g, kv1, farlat[1:])
+        attend(g, lined(g), nlat * step1, cols, step1, rows)
     finish(3)
     for s in range(nlon):
         done = back(1, att[...], s, width)
         out[:, :, s * width : (s + 1) * width] = done.reshape(cols, step1, width)[:, :rows, :]
-    for copy in pending + kv_sends:
+    for copy in pending + sum(kv_sends, []):
         copy.wait_send()
 
 
@@ -438,7 +443,6 @@
     tokens, qkv_weight = jnp.swapaxes(tokens, 0, 1), jnp.swapaxes(qkv_weight, 1, 2)
     cols, rows, feature = tokens.shape
     count = rows * 16
-    columns = 2 * KV * HD
     vmem = pl.BlockSpec(memory_space=pltpu.VMEM)
     hbm = pl.BlockSpec(memory_space=pl.ANY)
     dma = pltpu.SemaphoreType.DMA
@@ -462,18 +466,18 @@
             pltpu.VMEM((2, count, count), BF16),
             pltpu.VMEM((count, feature), BF16),
             pltpu.VMEM((count, feature), BF16),
-            pltpu.VMEM((cols, 32, columns), BF16),
-            pltpu.VMEM((nlon, cols, 32, columns), BF16),
-            pltpu.VMEM((nlat, cols, 32, columns), BF16),
-            pltpu.VMEM((nlon, count, columns), BF16),
+            pltpu.VMEM((KV, cols, 32, 2 * HD), BF16),
+            pltpu.VMEM((KV, nlon, cols, 32, 2 * HD), BF16),
+            pltpu.VMEM((KV, nlat, cols, 32, 2 * HD), BF16),
+            pltpu.VMEM((KV, nlon, count, 2 * HD), BF16),
             dma((4, nlon, PLANE)),
             dma((4, nlon)),
             dma((4, nlon, 4)),
             dma((4, nlon, 3)),
             dma((8,)),
             dma((8,)),
-            dma((2, max(nlat, nlon))),
-            dma((2, max(nlat, nlon))),
+            dma((2, KV, max(nlat, nlon))),
+            dma((2, KV, max(nlat, nlon))),
             dma((4,)),
         ],
         compiler_params=pltpu.CompilerParams(

time: 90 us -> 80 us (0.89)
  Pallas kernels: 87.6 us -> 77.9 us
    pallas_call x1, Pallas kernels: 87.6 us -> 77.9 us  [fused(): pl.pallas_call(functools.partial(step_kernel, nlat, nlon), out_shape=jax....]
where the time goes in v3:
time: 80 us; the launch traced here: 79.8 us
  Pallas kernels  77.9 us (97%)
  local copies, waits for them, and re-layouts  1.88 us (2%)
    pallas_call x1, Pallas kernels, fused(): pl.pallas_call(functools.partial(step_kernel, nlat, nlon), out_shape=jax....  77.9 us
    unnamed x1, local copies, waits for them, and re-layouts  1.88 us

profile of v3, /device:TPU:13, one launch (start us, length us, event | category | flops | bytes accessed | tf_op | source)
XLA Modules:
  0.0 79.8 jit_solution(2016892859586215685)
XLA Ops:
  0.0 77.9 %shard_map.64 = bf16[11,22,1024]{2,1,0:T(8,128)(2,1)} custom-call(bf16[11,22,1024]{2,1,0:T(8,128)(2,1)} %bitcast.5, bf16[2,320,1024]{2,1,0:T(8,128)(2,1)} %bitcast.4, bf16[2,1024,256]{2,1,0:T(8,128)(2,1)} %wo_in.1, f32[2,1024]{1,0:T(2,128)} %gain.1, bf16[9,1024]{1,0:T(8,128)(2,1)} %conv_w.1, bf16[1024]{0:T(1024)(128)(2,1)} %conv_b.1), custom_call_target="tpu_custom_call" | custom-call | tf_op jit(solution)/shard_map/pallas_call | solution.py:449
  77.9 1.9 %copy.8 = bf16[22,11,1024]{2,0,1:T(8,128)(2,1)} copy(bf16[22,11,1024]{2,0,1:T(8,128)(2,1)} %bitcast.3) | data formatting | bytes 991232

commit v4 on v3

--- a/solution.py
+++ b/solution.py
@@ -275,7 +275,7 @@
         normed[spot, :] = rms(rounded.astype(F32), 0)
         return carry
 
-    lax.fori_loop(0, cols, conv_line, 0)
+    lax.fori_loop(0, cols, conv_line, 0, unroll=True)
     to = lax.broadcasted_iota(jnp.int32, (count, 1), 0)
     fro = lax.broadcasted_iota(jnp.int32, (count, count), 1)
     turn[0] = jnp.where(
@@ -381,12 +381,13 @@
     share(0)
     spread(1)
     share_diagonal(0)
+    share(1)
     finish(0)
     for g in range(KV):
         send_kv(0, g, kv0, [(d, (ens, lat, far[d])) for d in range(1, nlon)], lon)
     spread(2)
     query_of(0, turned)
-    share(1)
+    share_diagonal(1)
 
     def gathered(g):
         return lambda spot: jnp.concatenate([kvt[g, s, spot, :] for s in range(nlon)], axis=0)
@@ -406,7 +407,6 @@
             ).astype(BF16)
         attend(g, gathered(g), nlon * step0, rows, step0, cols)
         if g == 0:
-            share_diagonal(1)
             share(2)
             spread(3)
     turned[...] = jnp.dot(turn[1], att[...], preferred_element_type=F32).astype(BF16)
@@ -422,7 +422,7 @@
         normed[spot, :] = rms(cur[spot, :].astype(F32), 1)
         return carry
 
-    lax.fori_loop(0, count // step1, norm_row, 0)
+    lax.fori_loop(0, count // step1, norm_row, 0, unroll=True)
     finish(2)
     for g in range(KV):
         send_kv(1, g, kv1, [(d, (ens, farlat[d], lon)) for d in range(1, nlat)], lat)

time: 80 us -> 79.2 us (0.990)
  Pallas kernels: 77.9 us -> 77.1 us
where the time goes in v4:
time: 79.2 us; the launch traced here: 79 us
  Pallas kernels  77.1 us (97%)
  local copies, waits for them, and re-layouts  1.88 us (2%)
    pallas_call x1, Pallas kernels, fused(): pl.pallas_call(functools.partial(step_kernel, nlat, nlon), out_shape=jax....  77.1 us
    unnamed x1, local copies, waits for them, and re-layouts  1.88 us

profile of v4, /device:TPU:13, one launch (start us, length us, event | category | flops | bytes accessed | tf_op | source)
XLA Modules:
  0.0 79.0 jit_solution(3257436612081206211)
XLA Ops:
  0.0 77.1 %shard_map.64 = bf16[11,22,1024]{2,1,0:T(8,128)(2,1)} custom-call(bf16[11,22,1024]{2,1,0:T(8,128)(2,1)} %bitcast.5, bf16[2,320,1024]{2,1,0:T(8,128)(2,1)} %bitcast.4, bf16[2,1024,256]{2,1,0:T(8,128)(2,1)} %wo_in.1, f32[2,1024]{1,0:T(2,128)} %gain.1, bf16[9,1024]{1,0:T(8,128)(2,1)} %conv_w.1, bf16[1024]{0:T(1024)(128)(2,1)} %conv_b.1), custom_call_target="tpu_custom_call" | custom-call | tf_op jit(solution)/shard_map/pallas_call | solution.py:449
  77.1 1.9 %copy.8 = bf16[22,11,1024]{2,0,1:T(8,128)(2,1)} copy(bf16[22,11,1024]{2,0,1:T(8,128)(2,1)} %bitcast.3) | data formatting | bytes 991232
